TPU v7x, 512 devices: a whole 4x4x16 slice. The times are simulated.
512 devices in a mesh: ax: 32 (over x_lo, z), az: 16 (over y, x_hi, core).
Axes of the slice: x: 4 (x_hi: 2, x_lo: 2; x = x_hi * 2 + x_lo), y: 4, z: 16, core: 2. Of those that a mesh axis runs over, the one named last changes fastest.
Arguments:
- conserved: float32 [5, 256, 1024, 128], P(None, 'ax', 'az'), may hold values from -0.6 to 3, as said below
- panel_cells: int32 [262144], P(('ax', 'az')), may hold values from 0 to 65535
- panel_counts: int32 [512], P(('ax', 'az')), may hold values from 1 to 512, 131072 in all
- time_bins: int32 [262144, 64], P(('ax', 'az')), may hold values from 0 to 1023
- amplitudes: float32 [262144, 64], P(('ax', 'az')), may hold values from 0.5 to 2
Outputs:
- section: float32 [5, 256, 1024, 128], P(None, 'ax', 'az')
- signal: float32 [64, 1024], P(None, ('ax', 'az'))
Inputs may be any that keep to these rules, and one draw needn't show every extreme that they name: `conserved`: component 0 lies in 0.7 to 1.3, components 1 to 3 in -0.6 to 0.6, component 4 in 2.0 to 3.0. `panel_counts`: some device has exactly 512 live panel slots, each device at least one.
All inputs are finite; a program needn't handle non-finite values.
Results may differ from a plain program's by a relative error of at most 0.000076.
Values sent between devices are 32-bit elements; how exact they have to be, the bound alone decides.
A program may use at most 64 MiB of HBM per device.

v0:
```python
import math
import jax
import jax.numpy as jnp
from jax import lax
from jax.sharding import PartitionSpec as P

AZIMUTH = 1024
CYCLES = 8
OBSERVERS = 64
BINS = 1024
gas_factor = 0.4
time_step = 0.02
ref_pressure = 0.95


def padded_2(value, sides, width, wrap):
    for axis, dim in sides:
        size, length = (lax.axis_size(axis), value.shape[dim])
        up = [(i, (i + 1) % size) for i in range(size if wrap else size - 1)]
        down = [(j, i) for i, j in up]
        last = lax.slice_in_dim(value, length - width, length, axis=dim)
        leading = lax.slice_in_dim(value, 0, width, axis=dim)
        before = lax.ppermute(last, axis, up)
        after = lax.ppermute(leading, axis, down)
        value = jnp.concatenate([before, value, after], axis=dim)
    return value


def primitives(conserved):
    fluid_rho_value = conserved[0]
    axial_vel = conserved[1] / fluid_rho_value
    radial_vel = conserved[2] / fluid_rho_value
    swirl_vel = conserved[3] / fluid_rho_value
    kinetic = 0.5 * (
        conserved[1] * axial_vel + conserved[2] * radial_vel + conserved[3] * swirl_vel
    )
    thermo_stress_level = gas_factor * (conserved[4] - kinetic)
    return jnp.stack([fluid_rho_value, axial_vel, radial_vel, swirl_vel, thermo_stress_level])


def flux_along(primitive, stream_heading):
    fluid_rho_value = primitive[0]
    thermo_stress_level = primitive[4]
    stream_speed = [primitive[1], primitive[2], primitive[3]]
    overall_heat_work = thermo_stress_level / gas_factor + 0.5 * fluid_rho_value * (
        stream_speed[0] * stream_speed[0]
        + stream_speed[1] * stream_speed[1]
        + stream_speed[2] * stream_speed[2]
    )
    holder_buffer = stream_speed[stream_heading]
    divided_pieces = [fluid_rho_value * holder_buffer]
    for entry_number in range(3):
        forcing_contribution = fluid_rho_value * stream_speed[entry_number] * holder_buffer
        if entry_number == stream_heading:
            forcing_contribution = forcing_contribution + thermo_stress_level
        divided_pieces.append(forcing_contribution)
    divided_pieces.append((overall_heat_work + thermo_stress_level) * holder_buffer)
    return jnp.stack(divided_pieces)


def fourth_diff(padded, along_axis, length):
    near_diff = lax.slice_in_dim(padded, 3, length + 3, axis=along_axis) - lax.slice_in_dim(
        padded, 1, length + 1, axis=along_axis
    )
    far_diff = lax.slice_in_dim(padded, 4, length + 4, axis=along_axis) - lax.slice_in_dim(
        padded, 0, length, axis=along_axis
    )
    return (8.0 * near_diff - far_diff) / 12.0


def cycle_weights(length):
    modes = jnp.arange(length // 2 + 1).astype(jnp.float32)
    cutoff = 4.0 * (jnp.arange(CYCLES).astype(jnp.float32) + 1.0)
    return jnp.exp(-((modes[None, :] / cutoff[:, None]) ** 8))


def apply_filter(line_block, cycle_index, length):
    half = length // 2 + 1
    sample = jnp.arange(length)
    modes = jnp.arange(half)
    phase = (sample[:, None] * modes[None, :] % length).astype(jnp.float32) * (
        2.0 * math.pi / length
    )
    cos_table = jnp.cos(phase)
    sin_table = jnp.sin(phase)
    factor = jnp.where((modes == 0) | (modes == length // 2), 1.0, 2.0) / length
    selector = (cycle_index[:, None] == jnp.arange(CYCLES)[None, :]).astype(jnp.float32)
    line_weight = (
        jnp.dot(selector, cycle_weights(length), precision=lax.Precision.HIGHEST) * factor[None, :]
    )
    real_part = jnp.einsum("fln,nm->flm", line_block, cos_table, precision=lax.Precision.HIGHEST)
    imag_part = jnp.einsum("fln,nm->flm", line_block, sin_table, precision=lax.Precision.HIGHEST)
    smooth = jnp.einsum(
        "flm,nm->fln", real_part * line_weight[None], cos_table, precision=lax.Precision.HIGHEST
    )
    smooth = smooth + jnp.einsum(
        "flm,nm->fln", imag_part * line_weight[None], sin_table, precision=lax.Precision.HIGHEST
    )
    return smooth


def on_device(conserved, panel_cells, panel_counts, time_bins, amplitudes):
    planes_dev = conserved.shape[1]
    sector = conserved.shape[2]
    radial_all = conserved.shape[3]
    primitive = primitives(conserved)
    radius = jnp.arange(radial_all).astype(jnp.float32) + 0.5
    dtheta = 2.0 * math.pi / AZIMUTH
    axial_flux = flux_along(primitive, 0)
    swirl_flux = flux_along(primitive, 2)
    padded_x = padded_2(axial_flux, (("ax", 1),), 2, False)
    padded_t = padded_2(swirl_flux, (("az", 2),), 2, True)
    radial_flux = flux_along(primitive, 1)
    padded_r = jnp.pad(radial_flux * radius, ((0, 0), (0, 0), (0, 0), (2, 2)))
    tendency = -fourth_diff(padded_x, 1, planes_dev)
    tendency = tendency - fourth_diff(padded_r, 3, radial_all) / radius
    tendency = tendency - fourth_diff(padded_t, 2, sector) / (radius * dtheta)
    fluid_rho_value = primitive[0]
    radial_vel = primitive[2]
    swirl_vel = primitive[3]
    thermo_stress_level = primitive[4]
    zeros_field = jnp.zeros_like(fluid_rho_value)
    source = jnp.stack(
        [
            zeros_field,
            zeros_field,
            (thermo_stress_level + fluid_rho_value * swirl_vel * swirl_vel) / radius,
            -fluid_rho_value * radial_vel * swirl_vel / radius,
            zeros_field,
        ]
    )
    raw_section = conserved + time_step * (tendency + source)
    inner = raw_section[..., :CYCLES]
    lines = jnp.transpose(inner, (0, 1, 3, 2)).reshape(5, planes_dev * CYCLES, sector)
    line_block = lax.all_to_all(lines, "az", split_axis=1, concat_axis=2, tiled=True)
    line_count = line_block.shape[1]
    cycle_index = (lax.axis_index("az") * line_count + jnp.arange(line_count)) % CYCLES
    smooth = apply_filter(line_block, cycle_index, AZIMUTH)
    filtered = lax.all_to_all(smooth, "az", split_axis=2, concat_axis=1, tiled=True)
    filtered = jnp.transpose(filtered.reshape(5, planes_dev, CYCLES, sector), (0, 1, 3, 2))
    section = jnp.concatenate([filtered, raw_section[..., CYCLES:]], axis=3)
    slot_count = panel_cells.shape[0]
    live = jnp.arange(slot_count) < panel_counts[0]
    sampled = jnp.where(live, thermo_stress_level.reshape(-1)[panel_cells] - ref_pressure, 0.0)
    contrib = sampled[:, None] * amplitudes
    segment = jnp.arange(OBSERVERS)[None, :] * BINS + time_bins
    partial_signal = jax.ops.segment_sum(
        contrib.reshape(-1), segment.reshape(-1), num_segments=OBSERVERS * BINS
    )
    signal = lax.psum_scatter(
        partial_signal.reshape(OBSERVERS, BINS), ("ax", "az"), scatter_dimension=1, tiled=True
    )
    return (section, signal)


def solution(mesh):
    placed = (
        P(None, "ax", "az", None),
        P(("ax", "az")),
        P(("ax", "az")),
        P(("ax", "az"), None),
        P(("ax", "az"), None),
    )
    return jax.shard_map(
        on_device,
        mesh=mesh,
        in_specs=placed,
        out_specs=(P(None, "ax", "az", None), P(None, ("ax", "az"))),
        check_vma=False,
    )
```

profile of v0, /device:TPU:4, one launch (start us, length us, event | category | flops | bytes accessed | tf_op | source)
XLA Modules:
  0.0 676.7 jit_solution(17818139211325658250)
XLA Ops:
  7.2 1.8 constant_dynamic-update-slice_fusion
  10.4 2.2 add_dynamic-update-slice_fusion.1
  12.6 1.0 fusion.89
  13.7 3.1 gather_fusion
  17.5 171.1 %scatter_custom_fusion = f32[65536]{0:T(1024)S(1)} fusion(s32[32768]{0:T(1024)S(1)} %reshape.97, f32[32768]{0:T(1024)S(1)} %reshape.99, f32[]{:T(128)} %constant.31.clone.1), kind=kCustom, calls=%fused_computation.96 | custom fusion | flops 32768 | bytes 262148 | tf_op jit(solution)/shard_map/scatter-add | solution.py:147
  189.4 0.8 multiply_dynamic-update-slice_fusion.5
  190.9 0.9 multiply_dynamic-update-slice_fusion.7
  191.8 1.0 multiply_dynamic-update-slice_fusion.4
  193.6 1.1 copy-done.2
  194.7 1.9 collective-permute-start.2
  197.3 2.4 collective-permute-start.3
  199.7 2.0 fusion.90
  201.7 1.3 collective-permute-start
  202.9 5.3 collective-permute-start.1
  210.6 0.9 broadcast_multiply_fusion
  213.6 4.0 multiply_add_fusion
  219.2 10.9 %all-to-all-start = ((f32[16,1,1280]{2,1,0:T(1,128)}), f32[16,1,1280]{2,1,0:T(1,128)S(1)}, u32[]{:S(2)}, u32[]{:S(2)}) async-start(f32[16,1,1280]{2,1,0:T(1,128)} %reshape.112), calls=%async_computation | async-start | bytes 163840 | tf_op jit(solution)/shard_map/all_to_all | solution.py:135
  230.3 4.7 all-to-all-done
  236.6 10.2 %fusion.45 = f32[5,4,513]{2,0,1:T(8,128)S(1)} fusion(f32[5,4,1024]{2,1,0:T(4,128)S(1)} %all_to_all.27, f32[4,513]{1,0:T(4,128)S(1)} %convolution_multiply_fusion), kind=kOutput, calls=%fused_computation.65 | convolution fusion | flops 133439504 | bytes 131168 | tf_op jit(solution)/shard_map/fln,nm->flm/dot_general | solution.py:92
  246.8 10.1 %fusion.42 = f32[5,4,513]{2,0,1:T(8,128)S(1)} fusion(f32[5,4,1024]{2,1,0:T(4,128)S(1)} %all_to_all.27, f32[4,513]{1,0:T(4,128)S(1)} %convolution_multiply_fusion), kind=kOutput, calls=%fused_computation.64 | convolution fusion | flops 133439504 | bytes 131168 | tf_op jit(solution)/shard_map/fln,nm->flm/dot_general | solution.py:91
  256.9 9.7 %fusion.3 = f32[5,4,1024]{2,0,1:T(8,128)S(1)} fusion(f32[5,4,513]{2,0,1:T(8,128)S(1)} %fusion.45), kind=kOutput, calls=%fused_computation.12 | convolution fusion | flops 133429248 | bytes 122960 | tf_op jit(solution)/shard_map/flm,nm->fln/dot_general | solution.py:96
  266.6 9.6 %fusion.39 = f32[5,4,1024]{2,0,1:T(8,128)S(1)} fusion(f32[5,4,1024]{2,0,1:T(8,128)S(1)} %fusion.3, f32[5,4,513]{2,0,1:T(8,128)S(1)} %fusion.42), kind=kOutput, calls=%fused_computation.63 | convolution fusion | flops 133449728 | bytes 204880 | tf_op jit(solution)/shard_map/flm,nm->fln/dot_general | solution.py:93
  276.2 1.8 copy.79
  277.9 4.4 reshape.114
  282.3 6.2 all-to-all-start.1
  288.5 371.6 %all-reduce.4.cloned.1.call-done = f32[64,1024]{1,0:T(8,128)} async-done(((f32[64,1024]{1,0:T(8,128)}), f32[64,1024]{1,0:T(8,128)}) %all-reduce.4.cloned.1.call-update) | async-done | bytes 262160
  660.1 0.8 constant_dynamic-slice_fusion
  662.0 0.8 reduce.1
  662.8 2.6 reshape.115
  665.4 1.6 copy.87
  667.0 1.0 copy.81
  668.4 1.5 pad_maximum_fusion.4
  (74 shorter events, 13.6 us)
Async XLA Ops:
  7.2 653.0 %all-reduce.4.cloned.1.call-start = ((), (), s32[]{:S(2)}) async-start(), calls=%async_computation.2 | async-start | bytes 524288
  10.4 2.2 copy-start
  13.7 3.2 copy-start.5
  13.7 3.4 copy-start.6
  189.4 1.5 copy-start.1
  189.4 4.2 copy-start.7
  193.6 1.1 copy-start.2
  193.6 17.0 %copy-start.4 = (f32[5,8,64,128]{3,2,1,0:T(8,128)S(1)}, f32[5,8,64,128]{3,2,1,0:T(8,128)}, u32[]{:S(2)}) copy-start(f32[5,8,64,128]{3,2,1,0:T(8,128)} %get-tuple-element.40) | copy-start | bytes 3932164
  194.7 17.4 %collective-permute-start.2 = (f32[5,8,2,128]{3,1,2,0:T(8,128)S(1)}, f32[5,8,2,128]{3,1,2,0:T(8,128)S(1)}, u32[]{:S(2)}, u32[]{:S(2)}) collective-permute-start(f32[5,8,2,128]{3,1,2,0:T(8,128)S(1)} %copy.70), channel_id=1, source_target_pairs={{1,0},{2,1},{3,2},{4,3},{5,4},{6,5},{7,6},{8,7},{9,8},{10,9},{11,1... | collective-permute-start | bytes 122888 | tf_op jit(solution)/shard_map/ppermute | solution.py:24
  197.3 14.9 %collective-permute-start.3 = (f32[5,8,2,128]{3,1,2,0:T(8,128)}, f32[5,8,2,128]{3,1,2,0:T(8,128)}, u32[]{:S(2)}, u32[]{:S(2)}) collective-permute-start(f32[5,8,2,128]{3,1,2,0:T(8,128)} %copy.72), channel_id=1, source_target_pairs={{0,1},{1,2},{2,3},{3,4},{4,5},{5,6},{6,7},{7,8},{8,9},{9,10},{10,1... | collective-permute-start | bytes 122888 | tf_op jit(solution)/shard_map/ppermute | solution.py:23
  201.7 11.3 %collective-permute-start = (f32[5,2,64,128]{3,2,1,0:T(8,128)}, f32[5,2,64,128]{3,2,1,0:T(8,128)S(1)}, u32[]{:S(2)}, u32[]{:S(2)}) collective-permute-start(f32[5,2,64,128]{3,2,1,0:T(8,128)} %get-tuple-element.35), channel_id=1, source_target_pairs={{16,0},{32,16},{48,32},{64,48},{80,64},{96,80},{112,96},{128,112},... | collective-permute-start | bytes 983048 | tf_op jit(solution)/shard_map/ppermute | solution.py:24
  202.9 10.7 %collective-permute-start.1 = (f32[5,2,64,128]{3,2,1,0:T(8,128)}, f32[5,2,64,128]{3,2,1,0:T(8,128)}, u32[]{:S(2)}, u32[]{:S(2)}) collective-permute-start(f32[5,2,64,128]{3,2,1,0:T(8,128)} %get-tuple-element.36), channel_id=1, source_target_pairs={{0,16},{16,32},{32,48},{48,64},{64,80},{80,96},{96,112},{112,128},... | collective-permute-start | bytes 983048 | tf_op jit(solution)/shard_map/ppermute | solution.py:23
  210.6 3.0 copy-start.3
  210.6 3.0 copy-start.8
  210.6 3.0 copy-start.11
  217.7 12.3 %copy-start.9 = (f32[513]{0:T(1024)S(1)}, f32[513]{0:T(1024)}, u32[]{:S(2)}) copy-start(f32[513]{0:T(1024)} %iota_convert_fusion) | copy-start | bytes 6160
  217.7 12.3 %copy-start.10 = (f32[513]{0:T(1024)S(1)}, f32[513]{0:T(1024)}, u32[]{:S(2)}) copy-start(f32[513]{0:T(1024)} %select_multiply_fusion) | copy-start | bytes 6160
  217.8 12.3 %copy-start.12 = (s32[4]{0:T(128)S(1)}, s32[4]{0:T(128)}, u32[]{:S(2)}) copy-start(s32[4]{0:T(128)} %and_select_fusion) | copy-start | bytes 52
  217.8 12.3 %copy-start.13 = (f32[8]{0:T(128)S(1)}, f32[8]{0:T(128)}, u32[]{:S(2)}) copy-start(f32[8]{0:T(128)} %add_multiply_fusion) | copy-start | bytes 100
  219.2 15.8 %all-to-all-start = ((f32[16,1,1280]{2,1,0:T(1,128)}), f32[16,1,1280]{2,1,0:T(1,128)S(1)}, u32[]{:S(2)}, u32[]{:S(2)}) async-start(f32[16,1,1280]{2,1,0:T(1,128)} %reshape.112), calls=%async_computation | async-start | bytes 163840 | tf_op jit(solution)/shard_map/all_to_all | solution.py:135
  282.3 379.7 %all-to-all-start.1 = ((f32[16,1,1280]{2,1,0:T(1,128)}), f32[16,1,1280]{2,1,0:T(1,128)S(1)}, u32[]{:S(2)}, u32[]{:S(2)}) async-start(f32[16,1,1280]{2,1,0:T(1,128)} %reshape.114), calls=%async_computation.1 | async-start | bytes 163840 | tf_op jit(solution)/shard_map/all_to_all | solution.py:139
Sparse Core Ops, SparseCore 0:
  189.5 470.5 all-reduce.3
where the time goes:
time: 677 us
  waiting for transfers between devices  377 us (56%)
  other arithmetic  191 us (28%)
  matrix products  39.7 us (6%)
  starting transfers between devices  28 us (4%)
  local copies, waits for them, and re-layouts  25.5 us (4%)
  between operations  15.1 us (2%)
    unnamed x2, waiting for transfers between devices  372 us
    scatter-add x1, other arithmetic, on_device(): jax.ops.segment_sum(contrib.reshape(-1), segment.reshape(-1), num_segment...  171 us
  transfers between devices with their start and end apart: 7, of which 3 were waited for; matrix products, arithmetic and copies ran while one was open for 10% of the time, Pallas kernels for 0%

commit v1 on v0

--- a/solution.py
+++ b/solution.py
@@ -11,6 +11,13 @@
 gas_factor = 0.4
 time_step = 0.02
 ref_pressure = 0.95
+
+
+def swap_blocks(x, axis, split, join):
+    size = lax.axis_size(axis)
+    blocks = jnp.stack(jnp.split(x, size, axis=split), axis=0)
+    blocks = lax.all_to_all(blocks, axis, split_axis=0, concat_axis=0)
+    return jnp.concatenate(blocks, axis=join)
 
 
 def padded_2(value, sides, width, wrap):
@@ -132,7 +139,7 @@
     raw_section = conserved + time_step * (tendency + source)
     inner = raw_section[..., :CYCLES]
     lines = jnp.transpose(inner, (0, 1, 3, 2)).reshape(5, planes_dev * CYCLES, sector)
-    line_block = lax.all_to_all(lines, "az", split_axis=1, concat_axis=2, tiled=True)
+    line_block = swap_blocks(lines, "az", 1, 2)
     line_count = line_block.shape[1]
     cycle_index = (lax.axis_index("az") * line_count + jnp.arange(line_count)) % CYCLES
     smooth = apply_filter(line_block, cycle_index, AZIMUTH)

time: 677 us -> 677 us (level)
  starting transfers between devices: 28 us -> 36.1 us
  transfers between devices with their start and end apart: 7 -> 7, of which waited for: 3 -> 3; matrix products, arithmetic and copies ran while one was open for 10% -> 9% of each run, Pallas kernels for 0% -> 0%
where the time goes in v1:
time: 677 us
  waiting for transfers between devices  374 us (55%)
  other arithmetic  187 us (28%)
  matrix products  39.7 us (6%)
  starting transfers between devices  36.1 us (5%)
  local copies, waits for them, and re-layouts  24.5 us (4%)
  between operations  15.3 us (2%)
    unnamed x2, waiting for transfers between devices  368 us
    scatter-add x1, other arithmetic, on_device(): jax.ops.segment_sum(contrib.reshape(-1), segment.reshape(-1), num_segment...  171 us
    all_to_all x1, starting transfers between devices, swap_blocks(): blocks = lax.all_to_all(blocks, axis, split_axis=0, concat_axis=0)  16.2 us
  transfers between devices with their start and end apart: 7, of which 3 were waited for; matrix products, arithmetic and copies ran while one was open for 9% of the time, Pallas kernels for 0%

profile of v1, /device:TPU:4, one launch (start us, length us, event | category | flops | bytes accessed | tf_op | source)
XLA Modules:
  0.0 676.8 jit_solution(9232927676452415728)
XLA Ops:
  8.7 1.0 broadcast_add_fusion
  9.9 1.8 constant_dynamic-update-slice_fusion
  11.7 0.9 add_dynamic-update-slice_fusion.1
  12.6 0.9 fusion.87
  13.6 3.1 gather_fusion
  17.1 171.1 %scatter_custom_fusion = f32[65536]{0:T(1024)S(1)} fusion(s32[32768]{0:T(1024)S(1)} %reshape.105, f32[32768]{0:T(1024)S(1)} %reshape.107, f32[]{:T(128)} %constant.31.clone.1), kind=kCustom, calls=%fused_computation.93 | custom fusion | flops 32768 | bytes 262148 | tf_op jit(solution)/shard_map/scatter-add | solution.py:154
  189.0 0.9 multiply_dynamic-update-slice_fusion.5
  190.4 0.9 multiply_dynamic-update-slice_fusion.7
  191.3 1.1 multiply_dynamic-update-slice_fusion.4
  192.5 2.1 fusion.88
  194.6 1.3 collective-permute-start
  195.8 5.3 collective-permute-start.1
  201.3 1.1 copy-done.3
  202.4 1.9 collective-permute-start.3
  204.3 5.1 collective-permute-start.2
  209.8 1.3 collective-permute-done.2
  211.2 4.2 multiply_add_fusion
  217.0 16.2 %all-to-all-start = ((f32[16,1,1280]{2,1,0:T(1,128)}), f32[16,1,1280]{2,1,0:T(1,128)S(1)}, u32[]{:S(2)}, u32[]{:S(2)}) async-start(f32[16,1,1280]{2,1,0:T(1,128)} %reshape.121), calls=%async_computation | async-start | bytes 163840 | tf_op jit(solution)/shard_map/all_to_all | solution.py:19
  233.4 4.7 all-to-all-done
  239.7 10.1 %fusion.45 = f32[5,4,513]{2,0,1:T(8,128)S(1)} fusion(f32[5,4,1024]{2,0,1:T(8,128)S(1)} %reshape.117, f32[4,513]{1,0:T(4,128)S(1)} %convolution_multiply_fusion), kind=kOutput, calls=%fused_computation.65 | convolution fusion | flops 133439504 | bytes 131168 | tf_op jit(solution)/shard_map/fln,nm->flm/dot_general | solution.py:99
  249.9 10.1 %fusion.42 = f32[5,4,513]{2,0,1:T(8,128)S(1)} fusion(f32[5,4,1024]{2,0,1:T(8,128)S(1)} %reshape.117, f32[4,513]{1,0:T(4,128)S(1)} %convolution_multiply_fusion), kind=kOutput, calls=%fused_computation.64 | convolution fusion | flops 133439504 | bytes 131168 | tf_op jit(solution)/shard_map/fln,nm->flm/dot_general | solution.py:98
  260.0 9.7 %fusion.3 = f32[5,4,1024]{2,0,1:T(8,128)S(1)} fusion(f32[5,4,513]{2,0,1:T(8,128)S(1)} %fusion.45), kind=kOutput, calls=%fused_computation.12 | convolution fusion | flops 133429248 | bytes 122960 | tf_op jit(solution)/shard_map/flm,nm->fln/dot_general | solution.py:103
  269.6 9.6 %fusion.39 = f32[5,4,1024]{2,0,1:T(8,128)S(1)} fusion(f32[5,4,1024]{2,0,1:T(8,128)S(1)} %fusion.3, f32[5,4,513]{2,0,1:T(8,128)S(1)} %fusion.42), kind=kOutput, calls=%fused_computation.63 | convolution fusion | flops 133449728 | bytes 204880 | tf_op jit(solution)/shard_map/flm,nm->fln/dot_general | solution.py:100
  279.2 1.8 copy.77
  281.0 4.4 reshape.123
  285.4 6.2 all-to-all-start.1
  291.6 368.3 %all-reduce.4.cloned.1.call-done = f32[64,1024]{1,0:T(8,128)} async-done(((f32[64,1024]{1,0:T(8,128)}), f32[64,1024]{1,0:T(8,128)}) %all-reduce.4.cloned.1.call-update) | async-done | bytes 262160
  659.9 0.8 constant_dynamic-slice_fusion
  661.3 1.5 slice.118
  663.6 2.6 reshape.124
  666.2 0.9 copy.84
  668.5 1.5 pad_maximum_fusion.4
  (80 shorter events, 9.2 us)
Async XLA Ops:
  7.2 4.5 copy-start
  7.2 652.7 %all-reduce.4.cloned.1.call-start = ((), (), s32[]{:S(2)}) async-start(), calls=%async_computation.2 | async-start | bytes 524288
  13.6 3.2 copy-start.8
  188.9 1.5 copy-start.2
  192.5 8.7 %copy-start.5 = (f32[5,8,64,128]{3,2,1,0:T(8,128)S(1)}, f32[5,8,64,128]{3,2,1,0:T(8,128)}, u32[]{:S(2)}) copy-start(f32[5,8,64,128]{3,2,1,0:T(8,128)} %get-tuple-element.18) | copy-start | bytes 3932164
  194.6 16.6 %collective-permute-start = (f32[5,2,64,128]{3,2,1,0:T(8,128)}, f32[5,2,64,128]{3,2,1,0:T(8,128)}, u32[]{:S(2)}, u32[]{:S(2)}) collective-permute-start(f32[5,2,64,128]{3,2,1,0:T(8,128)} %get-tuple-element.35), channel_id=1, source_target_pairs={{16,0},{32,16},{48,32},{64,48},{80,64},{96,80},{112,96},{128,112},... | collective-permute-start | bytes 983048 | tf_op jit(solution)/shard_map/ppermute | solution.py:31
  195.8 15.3 %collective-permute-start.1 = (f32[5,2,64,128]{3,2,1,0:T(8,128)}, f32[5,2,64,128]{3,2,1,0:T(8,128)}, u32[]{:S(2)}, u32[]{:S(2)}) collective-permute-start(f32[5,2,64,128]{3,2,1,0:T(8,128)} %get-tuple-element.36), channel_id=1, source_target_pairs={{0,16},{16,32},{32,48},{48,64},{64,80},{80,96},{96,112},{112,128},... | collective-permute-start | bytes 983048 | tf_op jit(solution)/shard_map/ppermute | solution.py:30
  201.3 1.1 copy-start.3
  202.4 7.4 %collective-permute-start.3 = (f32[5,8,2,128]{3,1,2,0:T(8,128)S(1)}, f32[5,8,2,128]{3,1,2,0:T(8,128)S(1)}, u32[]{:S(2)}, u32[]{:S(2)}) collective-permute-start(f32[5,8,2,128]{3,1,2,0:T(8,128)S(1)} %copy.71), channel_id=1, source_target_pairs={{0,1},{1,2},{2,3},{3,4},{4,5},{5,6},{6,7},{7,8},{8,9},{9,10},{10,1... | collective-permute-start | bytes 122888 | tf_op jit(solution)/shard_map/ppermute | solution.py:30
  204.3 6.8 %collective-permute-start.2 = (f32[5,8,2,128]{3,1,2,0:T(8,128)S(1)}, f32[5,8,2,128]{3,1,2,0:T(8,128)S(1)}, u32[]{:S(2)}, u32[]{:S(2)}) collective-permute-start(f32[5,8,2,128]{3,1,2,0:T(8,128)S(1)} %copy.69), channel_id=1, source_target_pairs={{1,0},{2,1},{3,2},{4,3},{5,4},{6,5},{7,6},{8,7},{9,8},{10,9},{11,1... | collective-permute-start | bytes 122888 | tf_op jit(solution)/shard_map/ppermute | solution.py:31
  209.5 1.6 copy-start.4
  209.5 1.6 copy-start.6
  209.5 1.6 copy-start.7
  217.0 21.2 %all-to-all-start = ((f32[16,1,1280]{2,1,0:T(1,128)}), f32[16,1,1280]{2,1,0:T(1,128)S(1)}, u32[]{:S(2)}, u32[]{:S(2)}) async-start(f32[16,1,1280]{2,1,0:T(1,128)} %reshape.121), calls=%async_computation | async-start | bytes 163840 | tf_op jit(solution)/shard_map/all_to_all | solution.py:19
  285.4 377.4 %all-to-all-start.1 = ((f32[16,1,1280]{2,1,0:T(1,128)}), f32[16,1,1280]{2,1,0:T(1,128)S(1)}, u32[]{:S(2)}, u32[]{:S(2)}) async-start(f32[16,1,1280]{2,1,0:T(1,128)} %reshape.123), calls=%async_computation.1 | async-start | bytes 163840 | tf_op jit(solution)/shard_map/all_to_all | solution.py:146
  667.2 1.3 copy-start.1
Sparse Core Ops, SparseCore 0:
  189.1 470.7 all-reduce.3
